TPU v7x, 32 devices: a whole 2x2x4 slice. The times are simulated.
32 devices in a mesh: cuts: 2 (over x), mode: 8 (over z, y), branch: 2 (over core).
Axes of the slice: x: 2, y: 2, z: 4, core: 2. Of those that a mesh axis runs over, the one named last changes fastest.
Arguments:
- leaves: bfloat16 [8, 2, 32, 512, 512], P('branch', None, ('cuts', 'mode')), parts along dimension 2, may hold values from -0.1875 to 0.1875
- join_order: int32 [7], replicated, may hold values from 0 to 1
- slice_values: int32 [32], P(('cuts', 'mode')), parts along dimension 0, may hold values from 0 to 1
- boundary: bfloat16 [2, 2, 512, 512], replicated, may hold values from -4 to 4
Outputs:
- amplitudes: float32 [2, 32, 512, 512], P(None, ('cuts', 'mode'), 'branch'), parts along dimension 1
There are 2 independent parts, one for each index of `cuts`. A program takes and returns all parts, laid end to end along the dimension named above; an argument that names none is the same for every part. Nothing has to cross between parts.
Inputs may be any that keep to these rules, and one draw needn't show every extreme that they name: `join_order`: 1 puts the second operand of the join on the left.
All inputs are finite; a program needn't handle non-finite values.
Results may differ from a plain program's by a relative error of at most 0.0076.
Values may be sent and summed in bfloat16 or wider, within the bound.
A program may use at most 64 MiB of HBM per device.

v0:
```python
import jax
import jax.numpy as jnp
from jax import lax
from jax.sharding import PartitionSpec as P


def from_partner(value, axis, bit):
    mask = 2**bit
    pairs = [(source, source ^ mask) for source in range(lax.axis_size(axis))]
    return lax.ppermute(value, axis, pairs)


def complex_sums(left_op, right_op):
    spec = "bij,bjk->bik"
    real_part = jnp.einsum(
        spec, left_op[0], right_op[0], preferred_element_type=jnp.float32
    ) - jnp.einsum(spec, left_op[1], right_op[1], preferred_element_type=jnp.float32)
    imag_part = jnp.einsum(
        spec, left_op[0], right_op[1], preferred_element_type=jnp.float32
    ) + jnp.einsum(spec, left_op[1], right_op[0], preferred_element_type=jnp.float32)
    return jnp.stack([real_part, imag_part])


def complex_product(left_op, right_op):
    return complex_sums(left_op, right_op).astype(jnp.bfloat16)


def join_pair(left_op, right_op, swapped):
    return lax.cond(
        swapped == 1,
        lambda: complex_product(right_op, left_op),
        lambda: complex_product(left_op, right_op),
    )


def split_rows(tensor, blocks):
    shape = tensor.shape
    return tensor.reshape(shape[0], shape[1], blocks, shape[2] // blocks, shape[3])


def merge_rows(tensor):
    shape = tensor.shape
    width = shape[4]
    total_rows = shape[1] * shape[2] * shape[3]
    return tensor.reshape(shape[0], total_rows // width, width, width)


def per_device(leaves, join_order, slice_values, boundary):
    blocks = lax.axis_size("mode")
    branch_index = lax.axis_index("branch")
    base_index = 2 * branch_index
    first_pair = join_pair(leaves[0], leaves[1], join_order[base_index])
    second_pair = join_pair(leaves[2], leaves[3], join_order[base_index + 1])
    first_pair, second_pair = (
        lax.all_to_all(
            split_rows(first_pair, blocks), "mode", split_axis=2, concat_axis=1, tiled=True
        ),
        lax.all_to_all(
            split_rows(second_pair, blocks), "mode", split_axis=2, concat_axis=1, tiled=True
        ),
    )
    first_pair = merge_rows(first_pair)
    second_pair = merge_rows(second_pair)
    middle = join_pair(first_pair, second_pair, join_order[4 + branch_index])
    middle = merge_rows(
        lax.all_to_all(split_rows(middle, blocks), "mode", split_axis=2, concat_axis=1, tiled=True)
    )
    width = middle.shape[3]
    half_rows = width // 2
    chosen = jnp.where(
        slice_values[None, :, None, None] == 1, boundary[1][:, None], boundary[0][:, None]
    )
    top_order = join_order[-1]
    partner = from_partner(middle, "branch", 0)
    is_first = branch_index == 0
    upper = jnp.where(is_first, middle, partner)
    lower = jnp.where(is_first, partner, middle)
    leading = jnp.where(top_order == 1, lower, upper)
    trailing = jnp.where(top_order == 1, upper, lower)
    leading = lax.dynamic_slice_in_dim(leading, branch_index * half_rows, half_rows, 2)
    top_half = complex_product(leading, trailing)
    amplitudes = complex_sums(top_half, chosen)
    return amplitudes


def solution(mesh):
    in_specs = (P("branch", None, ("cuts", "mode"), None, None), P(), P(("cuts", "mode")), P())
    out_specs = P(None, ("cuts", "mode"), "branch", None)
    return jax.shard_map(
        per_device, mesh=mesh, in_specs=in_specs, out_specs=out_specs, check_vma=False
    )
```

profile of v0, /device:TPU:0, one launch (start us, length us, event | category | flops | bytes accessed | tf_op | source)
XLA Modules:
  0.0 195.7 jit_solution(156778789101351986)
XLA Ops:
  0.0 5.7 %slice_bitcast_fusion = (bf16[2,2,512,512]{3,2,1,0:T(8,128)(2,1)}, bf16[2,2,512,512]{3,2,1,0:T(8,128)(2,1)S(1)}, bf16[2,2,512,512]{3,2,1,0:T(8,128)(2,1)}, bf16[2,2,512,512]{3,2,1,0:T(8,128)(2,1)}) fusion(bf16[4,2,2,512,512]{4,3,2,1,0:T(8,128)(2,1)} %param.10), kind=kLoop, calls=%fused_computation.127 | loop fusion | bytes 16777216 | tf_op jit(solution)/shard_map/squeeze | solution.py:53
  7.0 6.6 %conditional.7 = (bf16[2,2,512,512]{3,2,1,0:T(8,128)(2,1)}) conditional(s32[]{:T(128)} %bitcast.45, (bf16[2,2,512,512]{3,2,1,0:T(8,128)(2,1)}, bf16[2,2,512,512]{3,2,1,0:T(8,128)(2,1)}) %tuple.34, (bf16[2,2,512,512]{3,2,1,0:T(8,128)(2,1)}, bf16[2,2,512,512]{3,2,1,0:T(8,128)(2,1)}) %tuple.35), branch_computations={%region_2.0_spmd, %region_3.0_spmd} | conditional | flops 2150629376 | bytes 39845952
  7.1 2.4 %fusion.36 = f32[2,512,512]{2,1,0:T(8,128)S(1)} fusion(bf16[2,2,512,512]{3,2,1,0:T(8,128)(2,1)} %get-tuple-element.49, bf16[2,2,512,512]{3,2,1,0:T(8,128)(2,1)} %get-tuple-element.48), kind=kOutput, calls=%fused_computation.45 | convolution fusion | flops 536870912 | bytes 4194304 | tf_op jit(solution)/shard_map/cond/branch_0_fun/bij,bjk->bik/dot_general | solution.py:18
  11.3 0.7 subtract_bitcast_fusion.2
  12.1 1.6 pad_maximum_fusion.2
  13.6 3.2 %copy.11 = bf16[2,2,8,64,512]{4,3,1,0,2:T(8,128)(2,1)} copy(bf16[2,2,8,64,512]{4,3,2,1,0:T(8,128)(2,1)} %bitcast.213) | data formatting | bytes 4194304 | tf_op jit(solution)/shard_map/reshape | solution.py:38
  16.8 7.3 %all-to-all-start.1 = ((bf16[2,2,8,64,512]{4,3,1,0,2:T(8,128)(2,1)}), bf16[2,2,8,64,512]{4,3,1,0,2:T(8,128)(2,1)}, u32[]{:S(2)}, u32[]{:S(2)}) async-start(bf16[2,2,8,64,512]{4,3,1,0,2:T(8,128)(2,1)} %copy.11), calls=%async_computation.1 | async-start | bytes 4194304 | tf_op jit(solution)/shard_map/all_to_all | solution.py:58
  24.7 4.5 %conditional.6 = (bf16[2,2,512,512]{3,2,1,0:T(8,128)(2,1)S(1)}) conditional(s32[]{:T(128)} %bitcast.38, (bf16[2,2,512,512]{3,2,1,0:T(8,128)(2,1)}, bf16[2,2,512,512]{3,2,1,0:T(8,128)(2,1)S(1)}) %tuple.32, (bf16[2,2,512,512]{3,2,1,0:T(8,128)(2,1)S(1)}, bf16[2,2,512,512]{3,2,1,0:T(8,128)(2,1)}) %tuple.33), branch_computations={%region_0.0_spmd, %region_1.0_spmd} | conditional | flops 2150629376 | bytes 31457316
  24.8 2.1 %fusion.18 = f32[2,512,512]{2,1,0:T(8,128)S(1)} fusion(bf16[2,2,512,512]{3,2,1,0:T(8,128)(2,1)} %get-tuple-element.47, bf16[2,2,512,512]{3,2,1,0:T(8,128)(2,1)S(1)} %get-tuple-element.46), kind=kOutput, calls=%fused_computation.24 | convolution fusion | flops 536870912 | bytes 4194304 | tf_op jit(solution)/shard_map/cond/branch_1_fun/bij,bjk->bik/dot_general | solution.py:18
  28.3 0.7 subtract_bitcast_fusion.1
  29.2 1.5 copy.9
  30.7 41.7 %all-to-all-done.1 = bf16[2,2,8,64,512]{4,3,1,0,2:T(8,128)(2,1)} async-done(((bf16[2,2,8,64,512]{4,3,1,0,2:T(8,128)(2,1)}), bf16[2,2,8,64,512]{4,3,1,0,2:T(8,128)(2,1)}, u32[]{:S(2)}, u32[]{:S(2)}) %all-to-all-start.1) | async-done | bytes 2097184 | tf_op jit(solution)/shard_map/all_to_all | solution.py:58
  72.4 4.4 %all-to-all-start = ((bf16[2,2,8,64,512]{4,3,1,0,2:T(8,128)(2,1)}), bf16[2,2,8,64,512]{4,3,1,0,2:T(8,128)(2,1)}, u32[]{:S(2)}, u32[]{:S(2)}) async-start(bf16[2,2,8,64,512]{4,3,1,0,2:T(8,128)(2,1)} %copy.9), calls=%async_computation | async-start | bytes 4194304 | tf_op jit(solution)/shard_map/all_to_all | solution.py:55
  77.5 1.8 copy.12
  79.3 45.3 %all-to-all-done = bf16[2,2,8,64,512]{4,3,1,0,2:T(8,128)(2,1)} async-done(((bf16[2,2,8,64,512]{4,3,1,0,2:T(8,128)(2,1)}), bf16[2,2,8,64,512]{4,3,1,0,2:T(8,128)(2,1)}, u32[]{:S(2)}, u32[]{:S(2)}) %all-to-all-start) | async-done | bytes 2097184 | tf_op jit(solution)/shard_map/all_to_all | solution.py:55
  124.6 1.8 copy.10
  126.4 3.3 %conditional.8 = (bf16[2,2,512,512]{3,2,1,0:T(8,128)(2,1)S(1)}) conditional(s32[]{:T(128)} %bitcast.37, (bf16[2,2,512,512]{3,2,1,0:T(8,128)(2,1)S(1)}, bf16[2,2,512,512]{3,2,1,0:T(8,128)(2,1)S(1)}) %tuple.55, (bf16[2,2,512,512]{3,2,1,0:T(8,128)(2,1)S(1)}, bf16[2,2,512,512]{3,2,1,0:T(8,128)(2,1)S(1)}) %tuple.56), branch_computations={%region_4.0_spmd, %region_5.0_spmd} | conditional | flops 2150629376 | bytes 23068680
  127.2 0.7 add_bitcast_fusion.4
  129.9 51.8 %all_to_all.45 = bf16[2,2,8,64,512]{4,3,1,0,2:T(8,128)(2,1)S(1)} all-to-all(bf16[2,2,8,64,512]{4,3,1,0,2:T(8,128)(2,1)S(1)} %copy.13), channel_id=1, replica_groups=mesh['cuts'=2,'mode'=8,'branch'=2] {'mode'}, dimensions={2} | all-to-all | bytes 4194304 | tf_op jit(solution)/shard_map/all_to_all | solution.py:66
  181.7 1.5 copy.14
  183.9 1.7 slice_bitcast_fusion.9
  185.9 1.9 collective-permute-done
  187.8 2.6 %broadcast_select_fusion.3 = (bf16[2,2,512,512]{3,2,1,0:T(8,128)(2,1)S(1)}, bf16[2,2,512,512]{3,2,1,0:T(8,128)(2,1)S(1)}, bf16[2,2,512,512]{3,2,1,0:T(8,128)(2,1)S(1)}) fusion(pred[]{:T(512)} %bitcast.36, bf16[2,2,512,512]{3,2,1,0:T(8,128)(2,1)} %collective-permute-done, bf16[2,2,512,512]{3,2,1,0:T(8,128)(2,1)} %bitcast.59, pred[]{:T(512)S(6)} %eq.28), kind=kLoop, calls=%fused_computation.134 | loop fusion | flops 3145728 | bytes 10485762 | tf_op jit(solution)/shard_map/jit(_where)/select_n | solution.py:79
  194.2 1.5 pad_maximum_fusion.6
  (33 shorter events, 10.7 us)
Async XLA Ops:
  0.0 5.7 %copy-start.6 = (s32[7]{0:T(128)S(1)}, s32[7]{0:T(128)}, u32[]{:S(2)}) copy-start(s32[7]{0:T(128)} %param.11) | copy-start | bytes 88
  7.0 2.4 %copy-start.2 = (bf16[2,2,512,512]{3,2,1,0:T(8,128)(2,1)S(1)}, bf16[2,2,512,512]{3,2,1,0:T(8,128)(2,1)}, u32[]{:S(2)}) copy-start(bf16[2,2,512,512]{3,2,1,0:T(8,128)(2,1)} %get-tuple-element.49) | copy-start | bytes 6291460 | tf_op jit(solution)/shard_map/conditional.1
  7.1 2.8 %copy-start.4 = (bf16[2,2,512,512]{3,2,1,0:T(8,128)(2,1)S(1)}, bf16[2,2,512,512]{3,2,1,0:T(8,128)(2,1)}, u32[]{:S(2)}) copy-start(bf16[2,2,512,512]{3,2,1,0:T(8,128)(2,1)} %get-tuple-element.48) | copy-start | bytes 6291460 | tf_op jit(solution)/shard_map/conditional.1
  16.8 55.7 %all-to-all-start.1 = ((bf16[2,2,8,64,512]{4,3,1,0,2:T(8,128)(2,1)}), bf16[2,2,8,64,512]{4,3,1,0,2:T(8,128)(2,1)}, u32[]{:S(2)}, u32[]{:S(2)}) async-start(bf16[2,2,8,64,512]{4,3,1,0,2:T(8,128)(2,1)} %copy.11), calls=%async_computation.1 | async-start | bytes 4194304 | tf_op jit(solution)/shard_map/all_to_all | solution.py:58
  24.8 2.1 %copy-start.1 = (bf16[2,2,512,512]{3,2,1,0:T(8,128)(2,1)S(1)}, bf16[2,2,512,512]{3,2,1,0:T(8,128)(2,1)}, u32[]{:S(2)}) copy-start(bf16[2,2,512,512]{3,2,1,0:T(8,128)(2,1)} %get-tuple-element.47) | copy-start | bytes 6291460 | tf_op jit(solution)/shard_map/conditional
  72.4 52.2 %all-to-all-start = ((bf16[2,2,8,64,512]{4,3,1,0,2:T(8,128)(2,1)}), bf16[2,2,8,64,512]{4,3,1,0,2:T(8,128)(2,1)}, u32[]{:S(2)}, u32[]{:S(2)}) async-start(bf16[2,2,8,64,512]{4,3,1,0,2:T(8,128)(2,1)} %copy.9), calls=%async_computation | async-start | bytes 4194304 | tf_op jit(solution)/shard_map/all_to_all | solution.py:55
  181.7 2.2 %copy-start.7 = (s32[2]{0:T(128)S(1)}, s32[2]{0:T(128)}, u32[]{:S(2)}) copy-start(s32[2]{0:T(128)} %param.12) | copy-start | bytes 28
  183.3 4.5 %collective-permute-start = (bf16[2,2,512,512]{3,2,1,0:T(8,128)(2,1)}, bf16[2,2,512,512]{3,2,1,0:T(8,128)(2,1)}, u32[]{:S(2)}, u32[]{:S(2)}) collective-permute-start(bf16[2,2,512,512]{3,2,1,0:T(8,128)(2,1)} %bitcast.59), channel_id=1, source_target_pairs={{0,1},{1,0},{2,3},{3,2},{4,5},{5,4},{6,7},{7,6},{8,9},{9,8},{10,11... | collective-permute-start | bytes 6291464 | tf_op jit(solution)/shard_map/ppermute | solution.py:10
where the time goes:
time: 196 us
  waiting for transfers between devices  88.9 us (45%)
  blocking collectives  51.8 us (26%)
  local copies, waits for them, and re-layouts  18.6 us (9%)
  matrix products  15.1 us (8%)
  starting transfers between devices  11.7 us (6%)
  other arithmetic  6.63 us (3%)
  between operations  2.74 us (1%)
    all_to_all x1, blocking collectives, per_device(): lax.all_to_all(split_rows(middle, blocks), 'mode', split_axis=2, concat_a...  51.8 us
    all_to_all x1, waiting for transfers between devices, per_device(): lax.all_to_all(split_rows(first_pair, blocks), 'mode', split_axis=2, conc...  45.3 us
    all_to_all x1, waiting for transfers between devices, per_device(): lax.all_to_all(split_rows(second_pair, blocks), 'mode', split_axis=2, con...  41.7 us
    all_to_all x1, starting transfers between devices, per_device(): lax.all_to_all(split_rows(second_pair, blocks), 'mode', split_axis=2, con...  7.31 us
    dot_general x5, matrix products, complex_sums(): jnp.einsum(spec, left_op[0], right_op[1], preferred_element_type=jnp.floa...  6.06 us
    squeeze x1, local copies, waits for them, and re-layouts, per_device(): second_pair = join_pair(leaves[2], leaves[3], join_order[base_index + 1])  5.73 us
    reshape x3, local copies, waits for them, and re-layouts, split_rows(): tensor.reshape(shape[0], shape[1], blocks, shape[2] // blocks, shape[3])  4.91 us
    all_to_all x1, starting transfers between devices, per_device(): lax.all_to_all(split_rows(first_pair, blocks), 'mode', split_axis=2, conc...  4.35 us
  transfers between devices with their start and end apart: 3, of which 3 were waited for; matrix products, arithmetic and copies ran while one was open for 5% of the time, Pallas kernels for 0%

commit v1 on v0

--- a/solution.py
+++ b/solution.py
@@ -2,6 +2,7 @@
 import jax.numpy as jnp
 from jax import lax
 from jax.sharding import PartitionSpec as P
+from jax.lax import all_to_all, axis_size
 
 
 def from_partner(value, axis, bit):
@@ -55,8 +56,14 @@
         lax.all_to_all(
             split_rows(first_pair, blocks), "mode", split_axis=2, concat_axis=1, tiled=True
         ),
-        lax.all_to_all(
-            split_rows(second_pair, blocks), "mode", split_axis=2, concat_axis=1, tiled=True
+        jnp.concatenate(
+            all_to_all(
+                jnp.stack(jnp.split(split_rows(second_pair, blocks), axis_size("mode"), axis=2)),
+                "mode",
+                split_axis=0,
+                concat_axis=0,
+            ),
+            axis=1,
         ),
     )
     first_pair = merge_rows(first_pair)

time: 196 us -> 204 us (1.041)
  local copies, waits for them, and re-layouts: 18.6 us -> 27.4 us
    unnamed x4 -> x11, local copies, waits for them, and re-layouts: 0.01 us -> 11.7 us
    reshape x3 -> x2, local copies, waits for them, and re-layouts: 4.91 us -> 1.7 us  [split_rows(): tensor.reshape(shape[0], shape[1], blocks, shape[2] // blocks, shape[3])]
where the time goes in v1:
time: 204 us
  waiting for transfers between devices  88.8 us (44%)
  blocking collectives  51.8 us (25%)
  local copies, waits for them, and re-layouts  27.4 us (13%)
  matrix products  15.1 us (7%)
  starting transfers between devices  11.7 us (6%)
  other arithmetic  5.93 us (3%)
  between operations  2.75 us (1%)
    all_to_all x1, blocking collectives, per_device(): lax.all_to_all(split_rows(middle, blocks), 'mode', split_axis=2, concat_a...  51.8 us
    all_to_all x1, waiting for transfers between devices, per_device(): lax.all_to_all(split_rows(first_pair, blocks), 'mode', split_axis=2, conc...  45.4 us
    all_to_all x1, waiting for transfers between devices, per_device(): all_to_all(jnp.stack(jnp.split(split_rows(second_pair, blocks), axis_size...  41.8 us
    unnamed x11, local copies, waits for them, and re-layouts  11.7 us
    all_to_all x1, starting transfers between devices, per_device(): all_to_all(jnp.stack(jnp.split(split_rows(second_pair, blocks), axis_size...  7.31 us
    squeeze x1, local copies, waits for them, and re-layouts, per_device(): second_pair = join_pair(leaves[2], leaves[3], join_order[base_index + 1])  5.7 us
    dot_general x5, matrix products, complex_sums(): jnp.einsum(spec, left_op[0], right_op[0], preferred_element_type=jnp.floa...  4.68 us
    dot_general x5, matrix products, complex_sums(): jnp.einsum(spec, left_op[0], right_op[1], preferred_element_type=jnp.floa...  4.37 us
  transfers between devices with their start and end apart: 3, of which 3 were waited for; matrix products, arithmetic and copies ran while one was open for 5% of the time, Pallas kernels for 0%

profile of v1, /device:TPU:0, one launch (start us, length us, event | category | flops | bytes accessed | tf_op | source)
XLA Modules:
  0.0 203.8 jit_solution(6147217979707647763)
XLA Ops:
  0.0 5.7 %slice_bitcast_fusion = (bf16[2,2,512,512]{3,2,1,0:T(8,128)(2,1)}, bf16[2,2,512,512]{3,2,1,0:T(8,128)(2,1)S(1)}, bf16[2,2,512,512]{3,2,1,0:T(8,128)(2,1)}, bf16[2,2,512,512]{3,2,1,0:T(8,128)(2,1)}) fusion(bf16[4,2,2,512,512]{4,3,2,1,0:T(8,128)(2,1)} %param.10), kind=kLoop, calls=%fused_computation.127 | loop fusion | bytes 16777216 | tf_op jit(solution)/shard_map/squeeze | solution.py:54
  7.0 6.5 %conditional.12 = (bf16[2,2,8,64,512]{4,3,2,1,0:T(8,128)(2,1)}) conditional(s32[]{:T(128)} %bitcast.45, (bf16[2,2,512,512]{3,2,1,0:T(8,128)(2,1)}, bf16[2,2,512,512]{3,2,1,0:T(8,128)(2,1)}) %tuple.57, (bf16[2,2,512,512]{3,2,1,0:T(8,128)(2,1)}, bf16[2,2,512,512]{3,2,1,0:T(8,128)(2,1)}) %tuple.58), branch_computations={%region_2.0_spmd, %region_3.0_spmd} | conditional | flops 2150629376 | bytes 39845952 | solution.py:30
  7.0 2.4 %fusion.42 = f32[2,512,512]{2,1,0:T(8,128)S(1)} fusion(bf16[2,2,512,512]{3,2,1,0:T(8,128)(2,1)} %get-tuple-element.136, bf16[2,2,512,512]{3,2,1,0:T(8,128)(2,1)} %get-tuple-element.135), kind=kOutput, calls=%fused_computation.51 | convolution fusion | flops 536870912 | bytes 4194304 | tf_op jit(solution)/shard_map/cond/branch_0_fun/bij,bjk->bik/dot_general | solution.py:16
  13.5 1.7 fusion.123
  15.2 1.7 fusion.122
  16.9 1.7 fusion.121
  18.5 1.7 fusion.120
  20.2 1.7 fusion.119
  21.9 1.7 fusion.118
  23.6 1.7 fusion.117
  25.3 1.7 fusion.116
  26.9 7.3 %all-to-all-start.1 = ((bf16[8,2,2,1,64,512]{5,4,2,1,3,0:T(8,128)(2,1)}), bf16[8,2,2,1,64,512]{5,4,2,1,3,0:T(8,128)(2,1)}, u32[]{:S(2)}, u32[]{:S(2)}) async-start(bf16[8,2,2,1,64,512]{5,4,2,1,3,0:T(8,128)(2,1)} %fusion.116), calls=%async_computation.1 | async-start | bytes 4194304 | tf_op jit(solution)/shard_map/all_to_all | solution.py:60
  34.9 4.5 %conditional.5 = (bf16[2,2,512,512]{3,2,1,0:T(8,128)(2,1)S(1)}) conditional(s32[]{:T(128)} %bitcast.38, (bf16[2,2,512,512]{3,2,1,0:T(8,128)(2,1)}, bf16[2,2,512,512]{3,2,1,0:T(8,128)(2,1)S(1)}) %tuple.55, (bf16[2,2,512,512]{3,2,1,0:T(8,128)(2,1)S(1)}, bf16[2,2,512,512]{3,2,1,0:T(8,128)(2,1)}) %tuple.56), branch_computations={%region_0.0_spmd, %region_1.0_spmd} | conditional | flops 2150629376 | bytes 31457316
  34.9 2.1 %fusion.18 = f32[2,512,512]{2,1,0:T(8,128)S(1)} fusion(bf16[2,2,512,512]{3,2,1,0:T(8,128)(2,1)} %get-tuple-element.134, bf16[2,2,512,512]{3,2,1,0:T(8,128)(2,1)S(1)} %get-tuple-element.133), kind=kOutput, calls=%fused_computation.24 | convolution fusion | flops 536870912 | bytes 4194304 | tf_op jit(solution)/shard_map/cond/branch_1_fun/bij,bjk->bik/dot_general | solution.py:19
  40.8 41.8 %all-to-all-done.1 = bf16[8,2,2,1,64,512]{5,4,2,1,3,0:T(8,128)(2,1)} async-done(((bf16[8,2,2,1,64,512]{5,4,2,1,3,0:T(8,128)(2,1)}), bf16[8,2,2,1,64,512]{5,4,2,1,3,0:T(8,128)(2,1)}, u32[]{:S(2)}, u32[]{:S(2)}) %all-to-all-start.1) | async-done | bytes 2097184 | tf_op jit(solution)/shard_map/all_to_all | solution.py:60
  82.6 4.4 %all-to-all-start = ((bf16[2,2,8,64,512]{4,3,1,0,2:T(8,128)(2,1)}), bf16[2,2,8,64,512]{4,3,1,0,2:T(8,128)(2,1)}, u32[]{:S(2)}, u32[]{:S(2)}) async-start(bf16[2,2,8,64,512]{4,3,1,0,2:T(8,128)(2,1)} %copy.24), calls=%async_computation | async-start | bytes 4194304 | tf_op jit(solution)/shard_map/all_to_all | solution.py:56
  87.6 1.8 copy.33
  89.3 45.4 %all-to-all-done = bf16[2,2,8,64,512]{4,3,1,0,2:T(8,128)(2,1)} async-done(((bf16[2,2,8,64,512]{4,3,1,0,2:T(8,128)(2,1)}), bf16[2,2,8,64,512]{4,3,1,0,2:T(8,128)(2,1)}, u32[]{:S(2)}, u32[]{:S(2)}) %all-to-all-start) | async-done | bytes 2097184 | tf_op jit(solution)/shard_map/all_to_all | solution.py:56
  134.8 1.8 copy.25
  136.6 3.3 %conditional.13 = (bf16[2,2,512,512]{3,2,1,0:T(8,128)(2,1)S(1)}) conditional(s32[]{:T(128)} %bitcast.37, (bf16[2,2,512,512]{3,2,1,0:T(8,128)(2,1)S(1)}, bf16[2,2,512,512]{3,2,1,0:T(8,128)(2,1)S(1)}) %tuple.78, (bf16[2,2,512,512]{3,2,1,0:T(8,128)(2,1)S(1)}, bf16[2,2,512,512]{3,2,1,0:T(8,128)(2,1)S(1)}) %tuple.79), branch_computations={%region_4.0_spmd, %region_5.0_spmd} | conditional | flops 2150629376 | bytes 23068680
  140.1 51.8 %all_to_all.35 = bf16[2,2,8,64,512]{4,3,1,0,2:T(8,128)(2,1)S(1)} all-to-all(bf16[2,2,8,64,512]{4,3,1,0,2:T(8,128)(2,1)S(1)} %copy.34), channel_id=1, replica_groups=mesh['cuts'=2,'mode'=8,'branch'=2] {'mode'}, dimensions={2} | all-to-all | bytes 4194304 | tf_op jit(solution)/shard_map/all_to_all | solution.py:73
  192.9 1.7 slice_bitcast_fusion.9
  194.8 1.6 collective-permute-done
  196.5 2.0 broadcast_select_fusion.3
  (40 shorter events, 17.6 us)
Async XLA Ops:
  0.0 5.7 %copy-start.6 = (s32[7]{0:T(128)S(1)}, s32[7]{0:T(128)}, u32[]{:S(2)}) copy-start(s32[7]{0:T(128)} %param.11) | copy-start | bytes 88
  7.0 2.4 %copy-start.2 = (bf16[2,2,512,512]{3,2,1,0:T(8,128)(2,1)S(1)}, bf16[2,2,512,512]{3,2,1,0:T(8,128)(2,1)}, u32[]{:S(2)}) copy-start(bf16[2,2,512,512]{3,2,1,0:T(8,128)(2,1)} %get-tuple-element.136) | copy-start | bytes 6291460 | tf_op jit(solution)/shard_map/cond
  7.0 2.8 %copy-start.4 = (bf16[2,2,512,512]{3,2,1,0:T(8,128)(2,1)S(1)}, bf16[2,2,512,512]{3,2,1,0:T(8,128)(2,1)}, u32[]{:S(2)}) copy-start(bf16[2,2,512,512]{3,2,1,0:T(8,128)(2,1)} %get-tuple-element.135) | copy-start | bytes 6291460 | tf_op jit(solution)/shard_map/cond
  26.9 55.7 %all-to-all-start.1 = ((bf16[8,2,2,1,64,512]{5,4,2,1,3,0:T(8,128)(2,1)}), bf16[8,2,2,1,64,512]{5,4,2,1,3,0:T(8,128)(2,1)}, u32[]{:S(2)}, u32[]{:S(2)}) async-start(bf16[8,2,2,1,64,512]{5,4,2,1,3,0:T(8,128)(2,1)} %fusion.116), calls=%async_computation.1 | async-start | bytes 4194304 | tf_op jit(solution)/shard_map/all_to_all | solution.py:60
  34.9 2.1 %copy-start.1 = (bf16[2,2,512,512]{3,2,1,0:T(8,128)(2,1)S(1)}, bf16[2,2,512,512]{3,2,1,0:T(8,128)(2,1)}, u32[]{:S(2)}) copy-start(bf16[2,2,512,512]{3,2,1,0:T(8,128)(2,1)} %get-tuple-element.134) | copy-start | bytes 6291460 | tf_op jit(solution)/shard_map/conditional
  82.6 52.2 %all-to-all-start = ((bf16[2,2,8,64,512]{4,3,1,0,2:T(8,128)(2,1)}), bf16[2,2,8,64,512]{4,3,1,0,2:T(8,128)(2,1)}, u32[]{:S(2)}, u32[]{:S(2)}) async-start(bf16[2,2,8,64,512]{4,3,1,0,2:T(8,128)(2,1)} %copy.24), calls=%async_computation | async-start | bytes 4194304 | tf_op jit(solution)/shard_map/all_to_all | solution.py:56
  191.9 1.0 copy-start.7
  192.1 4.4 %collective-permute-start = (bf16[2,2,512,512]{3,2,1,0:T(8,128)(2,1)S(1)}, bf16[2,2,512,512]{3,2,1,0:T(8,128)(2,1)}, u32[]{:S(2)}, u32[]{:S(2)}) collective-permute-start(bf16[2,2,512,512]{3,2,1,0:T(8,128)(2,1)S(1)} %bitcast.254), channel_id=1, source_target_pairs={{0,1},{1,0},{2,3},{3,2},{4,5},{5,4},{6,7},{7,6},{8,9},{9,8},{10,11... | collective-permute-start | bytes 6291464 | tf_op jit(solution)/shard_map/ppermute | solution.py:11
